TPU v7x, 512 devices: a whole 4x4x16 slice. The times are simulated.
512 devices in a mesh: gx: 64 (over z, x_hi, core), col: 8 (over y, x_lo).
Axes of the slice: x: 4 (x_hi: 2, x_lo: 2; x = x_hi * 2 + x_lo), y: 4, z: 16, core: 2. Of those that a mesh axis runs over, the one named last changes fastest.
Arguments:
- field: bfloat16 [192, 2, 1024, 1024], P('col', None, 'gx'), may hold values from -6 to 6
- weights: bfloat16 [64, 64, 2, 192, 192], P('gx', None, None, None, 'col'), may hold values from -4 to 4
- bias: float32 [192], P('col'), may hold values from -1 to 1
Outputs:
- activated: bfloat16 [192, 2, 1024, 1024], P('col', None, 'gx')
All inputs are finite; a program needn't handle non-finite values.
Results may differ from a plain program's by a relative error of at most 0.0053.
Values may be sent and summed in bfloat16 or wider, within the bound.
A program may use at most 64 MiB of HBM per device.

v0:
```python
import functools
import math

import jax
import jax.numpy as jnp
import numpy as np
from jax import lax
from jax.experimental import pallas as pl
from jax.experimental.pallas import tpu as pltpu
from jax.sharding import PartitionSpec as P

MESH = pl.DeviceIdType.MESH
BF = jnp.bfloat16
F32 = jnp.float32

N = 1024
M = 64
S = 64
XL = 16
J = 8
CL = 24
PL = 2
H = CL * XL


def _bf(a):
    return np.asarray(a, np.float32).astype(jnp.bfloat16)


def _split(a):
    hi = _bf(a)
    return hi, _bf(np.asarray(a, np.float64) - hi.astype(np.float64))


@functools.cache
def tables():
    y = np.arange(N)
    ky = np.arange(M)
    ang = 2 * np.pi * ((ky[:, None] * y[None, :]) % N) / N
    sc = 1 / math.sqrt(N)
    yt = _bf(np.stack([np.cos(ang) * sc, -np.sin(ang) * sc], 1).reshape(2 * M, N))
    wgt = np.where(ky == 0, 1.0, 2.0)[:, None]
    g = np.stack([wgt * np.cos(ang) * sc, -wgt * np.sin(ang) * sc], 1).reshape(2 * M, N)
    g2 = np.concatenate(_split(g), 0)

    k = np.arange(M)
    s = np.arange(S)
    ph = 2 * np.pi * ((k[:, None] * s[None, :]) % S) / S
    c, d = np.cos(ph) * sc, np.sin(ph) * sc
    dm = np.zeros((2, M, S, 2))
    dm[0, :, :, 0], dm[0, :, :, 1] = c, d
    dm[1, :, :, 0], dm[1, :, :, 1] = -d, c
    d2 = np.concatenate(_split(dm.reshape(2 * M, 2 * S)), 1)

    f = np.where(k < M // 2, k, k - M)
    tw = 2 * np.pi * f[:, None] * np.arange(XL)[None, :] / N
    tct = np.tile(np.cos(tw), (1, 8))
    tst = np.tile(np.sin(tw), (1, 8))

    bt = np.zeros((CL, CL, XL), np.float32)
    ex = np.zeros((2, 2, CL, 2, CL, XL), np.float32)
    for o in range(CL):
        bt[o, o] = 1
        for w in range(2):
            ex[:, w, o, w, o, :] = 1
    bt = _bf(bt.reshape(CL, H))
    ex = _bf(ex.reshape(4 * CL, 2 * H))

    e = np.zeros((S, 2, 2, 2, M))
    for ab in range(2):
        for r in range(2):
            val = np.exp(1j * ph.T) * (1j ** (r + ab)) * sc
            e[:, 0, ab, r] = val.real
            e[:, 1, ab, r] = val.imag
    ehi, elo = _split(e.reshape(2 * S, 256))
    ee = np.concatenate([ehi, elo], 0)
    tf = np.concatenate([tct, tst], 0).astype(np.float32)
    return dict(yt=yt, g2=g2, d2=d2, tf=tf, bt=bt, ex=ex, ee=ee)


def split(v):
    hi = v.astype(BF)
    return hi, (v - hi.astype(F32)).astype(BF)


def dot(a, b):
    return jnp.dot(a, b, preferred_element_type=F32)


def dot_nt(a, b):
    return lax.dot_general(a, b, (((1,), (1,)), ((), ())), preferred_element_type=F32)


NAMES = ("yt", "d2", "tf", "bt", "ex", "ee", "g2")


def exchange_kernel(*refs):
    nt = len(NAMES)
    field_h, w_h, bias_h = refs[:3]
    tabs_h = refs[3:3 + nt]
    out_h = refs[3 + nt]
    fbuf, wbuf, bias_s = refs[4 + nt:7 + nt]
    tabs = dict(zip(NAMES, refs[7 + nt:7 + 2 * nt]))
    (send1, recv1, ags, agr, send2, recv2, obuf,
     in_sem, loc_sem, s1, r1, sa, ra, s2, r2, out_sem) = refs[7 + 2 * nt:]

    me = lax.axis_index("gx")
    mc = lax.axis_index("col")

    first = [pltpu.make_async_copy(tabs_h[0], tabs["yt"], in_sem.at[0])]
    first += [pltpu.make_async_copy(field_h.at[:, p], fbuf.at[p], in_sem.at[1 + p]) for p in range(PL)]
    rest = [pltpu.make_async_copy(h, tabs[n], in_sem.at[5 + i])
            for i, (h, n) in enumerate(zip(tabs_h[1:], NAMES[1:]))]
    rest += [pltpu.make_async_copy(w_h, wbuf, in_sem.at[3]),
             pltpu.make_async_copy(bias_h, bias_s, in_sem.at[4])]
    for c in first:
        c.start()

    barrier = pltpu.get_barrier_semaphore()

    def hello(axis, t):
        pl.semaphore_signal(barrier, inc=1, device_id={axis: t}, device_id_type=MESH)

    def around(go):
        go(lax.rem(me + S // 2, S))

        def pair(i, _):
            go(lax.rem(me + S // 2 - i, S))
            go(lax.rem(me + S // 2 + i, S))
            return 0

        lax.fori_loop(1, S // 2, pair, 0)

    def greet_col(i, _):
        hello("col", lax.rem(mc + i, J))
        return 0

    around(lambda t: hello("gx", t))
    lax.fori_loop(1, J, greet_col, 0)
    for c in rest:
        c.start()
    first[0].wait()
    for p in range(PL):
        first[1 + p].wait()
        h = dot_nt(tabs["yt"][...], fbuf[p].reshape(H, N))
        send1[p] = h.astype(BF).reshape(S, 2, H)

    pl.semaphore_wait(barrier, S - 1 + J - 1)

    def message(t, slot, send, recv, ssem, rsem):
        return pltpu.make_async_remote_copy(
            src_ref=send.at[t], dst_ref=recv.at[slot], send_sem=ssem.at[t], recv_sem=rsem.at[slot],
            device_id={"gx": t}, device_id_type=MESH)

    def exchange(*refs):
        own = pltpu.make_async_copy(refs[0].at[me], refs[1].at[me], loc_sem)
        own.start()
        around(lambda t: message(t, me, *refs).start())
        own.wait()

    def others(wait):
        def one(i, _):
            wait(lax.rem(me + i, S))
            return 0

        lax.fori_loop(1, S, one, 0)

    def arrive(*refs):
        others(lambda t: message(t, t, *refs).wait_recv())

    def drain(*refs):
        others(lambda t: message(t, t, *refs).wait_send())

    def port(send, recv, ssem, rsem, p):
        return send.at[p], recv.at[p], ssem.at[p], rsem.at[p]

    ports1 = [port(send1, recv1, s1, r1, p) for p in range(PL)]
    ports2 = [port(send2, recv2, s2, r2, p) for p in range(PL)]

    def columns(wait, p):
        def one(i, _):
            t = lax.rem(mc + i, J)
            slot = mc if wait is None else t
            c = pltpu.make_async_remote_copy(
                src_ref=ags.at[p], dst_ref=agr.at[p, slot], send_sem=sa.at[p, t], recv_sem=ra.at[p, slot],
                device_id={"col": t}, device_id_type=MESH)
            if wait is None:
                c.start()
            elif wait:
                c.wait_recv()
            else:
                c.wait_send()
            return 0

        lax.fori_loop(1, J, one, 0)

    for p in range(PL):
        exchange(*ports1[p])
    for c in rest:
        c.wait()

    tc = jnp.concatenate([tabs["tf"][0:M]] * 3, 1)
    ts = jnp.concatenate([tabs["tf"][M:2 * M]] * 3, 1)
    for p in range(PL):
        arrive(*ports1[p])
        got = recv1[p].reshape(2 * S, H)
        g = dot(tabs["d2"][...], jnp.concatenate([got, got], 0))
        gr, gi = g[:M], g[M:]
        hi, lo = split(jnp.concatenate([tc * gr + ts * gi, tc * gi - ts * gr], 0))
        bt = tabs["bt"][...]
        ags[p] = (dot_nt(bt, hi) + dot_nt(bt, lo)).astype(BF)
        own = pltpu.make_async_copy(ags.at[p], agr.at[p, mc], loc_sem)
        own.start()
        columns(None, p)
        own.wait()

    lane = lax.broadcasted_iota(jnp.int32, (2 * CL, 2 * M), 1) % M
    tc = jnp.concatenate([tc, tc], 0)
    ts = jnp.concatenate([ts, ts], 0)
    for p in range(PL):
        columns(True, p)
        a = agr[p].reshape(J * CL, 2 * M)
        mixed = jnp.zeros((2 * CL, 2 * M), F32)
        for kg in range(8):
            z = dot(wbuf[384 * kg:384 * kg + 384, :], a)
            for i in range(8):
                mixed = jnp.where(lane == 8 * kg + i, z[48 * i:48 * i + 48], mixed)
        hi, lo = split(mixed)
        y = lax.dot_general(jnp.concatenate([hi, lo], 0), tabs["ex"][...], (((0,), (0,)), ((), ())),
                            preferred_element_type=F32)
        y0, y1 = y[:, :H], y[:, H:]
        hi, lo = split(jnp.concatenate([tc * y0 - ts * y1, tc * y1 + ts * y0], 0))
        ee = tabs["ee"]
        wide = dot(ee[:128], hi) + dot(ee[128:], hi) + dot(ee[:128], lo)
        send2[p] = wide.astype(BF).reshape(S, 2, H)
        exchange(*ports2[p])

    for p in range(PL):
        drain(*ports1[p])
        columns(False, p)
    g2 = tabs["g2"]
    ob = 8
    puts = []
    for p in range(PL):
        arrive(*ports2[p])
        got = recv2[p].reshape(2 * S, H)
        got = jnp.concatenate([got, got], 0)
        for n in range(CL // ob):
            v = lax.dot_general(got[:, 128 * n:128 * n + 128], g2[...], (((0,), (0,)), ((), ())),
                                preferred_element_type=F32)
            for i in range(ob):
                o = n * ob + i
                u = v[XL * i:XL * i + XL] + bias_s[o]
                u = 0.5 * u * (1.0 + lax.erf(u * math.sqrt(0.5)))
                obuf[p, o] = u.astype(BF)
            put = pltpu.make_async_copy(
                obuf.at[p, pl.ds(n * ob, ob)], out_h.at[pl.ds(n * ob, ob), p], out_sem.at[p, n])
            put.start()
            puts.append(put)
    for p in range(PL):
        drain(*ports2[p])
    for put in puts:
        put.wait()


def exchanges(field, w, bias, tabs):
    ops = [tabs[n] for n in NAMES]
    vm = [pltpu.VMEM((PL, CL, XL, N), BF), pltpu.VMEM((M * 2 * CL, J * CL), BF), pltpu.SMEM((CL,), F32)]
    vm += [pltpu.VMEM(t.shape, t.dtype) for t in ops]
    msg = pltpu.VMEM((PL, S, 2, H), BF)
    dma = pltpu.SemaphoreType.DMA
    return pl.pallas_call(
        exchange_kernel,
        out_shape=jax.ShapeDtypeStruct((CL, PL, XL, N), BF),
        in_specs=[pl.BlockSpec(memory_space=pl.ANY)] * (3 + len(ops)),
        out_specs=pl.BlockSpec(memory_space=pl.ANY),
        scratch_shapes=vm + [
            msg, msg, pltpu.VMEM((PL, CL, 2 * M), BF), pltpu.VMEM((PL, J, CL, 2 * M), BF), msg, msg,
            pltpu.VMEM((PL, CL, XL, N), BF),
            dma((4 + len(ops),)), dma,
            dma((PL, S)), dma((PL, S)), dma((PL, J)), dma((PL, J)), dma((PL, S)), dma((PL, S)), dma((PL, 3))],
        compiler_params=pltpu.CompilerParams(
            collective_id=0, has_side_effects=True, vmem_limit_bytes=67043328),
        name="exchange",
    )(field, w, bias, *ops)


def body(field, weights, bias):
    tabs = {n: jnp.asarray(t) for n, t in tables().items()}
    w = jnp.swapaxes(weights, 3, 4).reshape(M * 2 * CL, J * CL)
    return exchanges(field, w, bias, tabs)


def solution(mesh):
    placed = (P("col", None, "gx", None), P("gx", None, None, None, "col"), P("col"))
    return jax.shard_map(
        body, mesh=mesh, in_specs=placed, out_specs=P("col", None, "gx", None), check_vma=False
    )
```

profile of v0, /device:TPU:1, one launch (start us, length us, event | category | flops | bytes accessed | tf_op | source)
XLA Modules:
  0.0 57.8 jit_solution(10744604993740399645)
XLA Ops:
  0.0 55.0 %exchange.1 = bf16[24,2,16,1024]{3,2,1,0:T(8,128)(2,1)} custom-call(bf16[24,2,16,1024]{3,2,1,0:T(8,128)(2,1)} %refs_0_.1, bf16[3072,192]{1,0:T(8,128)(2,1)} %bitcast.3, f32[24]{0:T(128)} %refs_2_.1, bf16[128,1024]{1,0:T(8,128)(2,1)} %constant.14.clone.refs_3_, bf16[128,256]{1,0:T(8,128)(2,1)} %constant.16.clone.refs_4_, f32[128,128]{1,0:T(8,128)} %constant.17.clone.refs_5_, ...), custom_call_target="tpu_custom_call" | custom-call | tf_op jit(solution)/shard_map/exchange/pallas_call | solution.py:272
  55.0 2.8 %copy.12 = bf16[24,2,16,1024]{3,2,1,0:T(8,128)(2,1)} copy(bf16[24,2,16,1024]{3,2,1,0:T(8,128)(2,1)} %exchange.1) | data formatting | bytes 3145728
where the time goes:
time: 57.9 us; the launch traced here: 57.8 us
  Pallas kernels  55 us (95%)
  local copies, waits for them, and re-layouts  2.77 us (5%)
    pallas_call x1, Pallas kernels, exchanges(): pl.pallas_call(exchange_kernel, out_shape=jax.ShapeDtypeStruct((CL, PL, X...  55 us
    unnamed x1, local copies, waits for them, and re-layouts  2.77 us

commit v1 on v0

--- a/solution.py
+++ b/solution.py
@@ -124,12 +124,16 @@
     def around(go):
         go(lax.rem(me + S // 2, S))
 
-        def pair(i, _):
-            go(lax.rem(me + S // 2 - i, S))
-            go(lax.rem(me + S // 2 + i, S))
+        def step(i, _):
+            for n in range(3):
+                d = 3 * i + n + 1
+                go(lax.rem(me + S // 2 - d, S))
+                go(lax.rem(me + S // 2 + d, S))
             return 0
 
-        lax.fori_loop(1, S // 2, pair, 0)
+        lax.fori_loop(0, 10, step, 0)
+        go(lax.rem(me + 1, S))
+        go(lax.rem(me + S - 1, S))
 
     def greet_col(i, _):
         hello("col", lax.rem(mc + i, J))
@@ -147,29 +151,28 @@
 
     pl.semaphore_wait(barrier, S - 1 + J - 1)
 
-    def message(t, slot, send, recv, ssem, rsem):
+    def message(t, send, recv, ssem, rsem):
         return pltpu.make_async_remote_copy(
-            src_ref=send.at[t], dst_ref=recv.at[slot], send_sem=ssem.at[t], recv_sem=rsem.at[slot],
+            src_ref=send.at[t], dst_ref=recv.at[me], send_sem=ssem, recv_sem=rsem,
             device_id={"gx": t}, device_id_type=MESH)
 
     def exchange(*refs):
         own = pltpu.make_async_copy(refs[0].at[me], refs[1].at[me], loc_sem)
         own.start()
-        around(lambda t: message(t, me, *refs).start())
+        around(lambda t: message(t, *refs).start())
         own.wait()
 
-    def others(wait):
-        def one(i, _):
-            wait(lax.rem(me + i, S))
-            return 0
-
-        lax.fori_loop(1, S, one, 0)
+    def others(send, recv, ssem, rsem):
+        every = pl.ds(0, S - 1)
+        return pltpu.make_async_remote_copy(
+            src_ref=send.at[every], dst_ref=recv.at[every], send_sem=ssem, recv_sem=rsem,
+            device_id={"gx": lax.rem(me + 1, S)}, device_id_type=MESH)
 
     def arrive(*refs):
-        others(lambda t: message(t, t, *refs).wait_recv())
+        others(*refs).wait_recv()
 
     def drain(*refs):
-        others(lambda t: message(t, t, *refs).wait_send())
+        others(*refs).wait_send()
 
     def port(send, recv, ssem, rsem, p):
         return send.at[p], recv.at[p], ssem.at[p], rsem.at[p]
@@ -177,22 +180,24 @@
     ports1 = [port(send1, recv1, s1, r1, p) for p in range(PL)]
     ports2 = [port(send2, recv2, s2, r2, p) for p in range(PL)]
 
-    def columns(wait, p):
+    def columns(p):
+        own = pltpu.make_async_copy(ags.at[p], agr.at[p, mc], loc_sem)
+        own.start()
+
         def one(i, _):
-            t = lax.rem(mc + i, J)
-            slot = mc if wait is None else t
-            c = pltpu.make_async_remote_copy(
-                src_ref=ags.at[p], dst_ref=agr.at[p, slot], send_sem=sa.at[p, t], recv_sem=ra.at[p, slot],
-                device_id={"col": t}, device_id_type=MESH)
-            if wait is None:
-                c.start()
-            elif wait:
-                c.wait_recv()
-            else:
-                c.wait_send()
+            pltpu.make_async_remote_copy(
+                src_ref=ags.at[p], dst_ref=agr.at[p, mc], send_sem=sa.at[p], recv_sem=ra.at[p],
+                device_id={"col": lax.rem(mc + i, J)}, device_id_type=MESH).start()
             return 0
 
         lax.fori_loop(1, J, one, 0)
+        own.wait()
+
+    def column_bytes(p):
+        every = agr.at[p, pl.ds(0, J - 1)]
+        return pltpu.make_async_remote_copy(
+            src_ref=every, dst_ref=every, send_sem=sa.at[p], recv_sem=ra.at[p],
+            device_id={"col": lax.rem(mc + 1, J)}, device_id_type=MESH)
 
     for p in range(PL):
         exchange(*ports1[p])
@@ -209,16 +214,13 @@
         hi, lo = split(jnp.concatenate([tc * gr + ts * gi, tc * gi - ts * gr], 0))
         bt = tabs["bt"][...]
         ags[p] = (dot_nt(bt, hi) + dot_nt(bt, lo)).astype(BF)
-        own = pltpu.make_async_copy(ags.at[p], agr.at[p, mc], loc_sem)
-        own.start()
-        columns(None, p)
-        own.wait()
+        columns(p)
 
     lane = lax.broadcasted_iota(jnp.int32, (2 * CL, 2 * M), 1) % M
     tc = jnp.concatenate([tc, tc], 0)
     ts = jnp.concatenate([ts, ts], 0)
     for p in range(PL):
-        columns(True, p)
+        column_bytes(p).wait_recv()
         a = agr[p].reshape(J * CL, 2 * M)
         mixed = jnp.zeros((2 * CL, 2 * M), F32)
         for kg in range(8):
@@ -237,7 +239,7 @@
 
     for p in range(PL):
         drain(*ports1[p])
-        columns(False, p)
+        column_bytes(p).wait_send()
     g2 = tabs["g2"]
     ob = 8
     puts = []
@@ -278,11 +280,11 @@
             msg, msg, pltpu.VMEM((PL, CL, 2 * M), BF), pltpu.VMEM((PL, J, CL, 2 * M), BF), msg, msg,
             pltpu.VMEM((PL, CL, XL, N), BF),
             dma((4 + len(ops),)), dma,
-            dma((PL, S)), dma((PL, S)), dma((PL, J)), dma((PL, J)), dma((PL, S)), dma((PL, S)), dma((PL, 3))],
+            dma((PL,)), dma((PL,)), dma((PL,)), dma((PL,)), dma((PL,)), dma((PL,)), dma((PL, 3))],
         compiler_params=pltpu.CompilerParams(
-            collective_id=0, has_side_effects=True, vmem_limit_bytes=67043328),
+            collective_id=0, has_side_effects=True, vmem_limit_bytes=24 * 2**20),
         name="exchange",
-    )(field, w, bias, *ops)
+    )(*[pltpu.with_memory_space_constraint(v, pltpu.HBM) for v in (field, w, bias, *ops)])
 
 
 def body(field, weights, bias):

time: 57.9 us -> 49.9 us (0.86)
  Pallas kernels: 55 us -> 48.6 us
  local copies, waits for them, and re-layouts: 2.77 us -> 1.15 us
    pallas_call x1, Pallas kernels: 55 us -> 48.6 us  [exchanges(): pl.pallas_call(exchange_kernel, out_shape=jax.ShapeDtypeStruct((CL, PL, X...]
    unnamed x1, local copies, waits for them, and re-layouts: 2.77 us -> 1.15 us
where the time goes in v1:
time: 49.9 us; the launch traced here: 49.8 us
  Pallas kernels  48.6 us (97%)
  local copies, waits for them, and re-layouts  1.15 us (2%)
    pallas_call x1, Pallas kernels, exchanges(): pl.pallas_call(exchange_kernel, out_shape=jax.ShapeDtypeStruct((CL, PL, X...  48.6 us
    unnamed x1, local copies, waits for them, and re-layouts  1.15 us

profile of v1, /device:TPU:1, one launch (start us, length us, event | category | flops | bytes accessed | tf_op | source)
XLA Modules:
  0.0 49.8 jit_solution(17239175420216386256)
XLA Ops:
  0.0 48.6 %exchange.1 = bf16[24,2,16,1024]{3,2,1,0:T(8,128)(2,1)S(1)} custom-call(bf16[24,2,16,1024]{3,2,1,0:T(8,128)(2,1)} %refs_0_.1, bf16[3072,192]{1,0:T(8,128)(2,1)} %bitcast.3, f32[24]{0:T(128)} %refs_2_.1, bf16[128,1024]{1,0:T(8,128)(2,1)} %constant.14.clone.refs_3_, bf16[128,256]{1,0:T(8,128)(2,1)} %constant.16.clone.refs_4_, ...), custom_call_target="tpu_custom_call" | custom-call | tf_op jit(solution)/shard_map/exchange/pallas_call | solution.py:274
  48.6 1.1 %copy.12 = bf16[24,2,16,1024]{3,2,1,0:T(8,128)(2,1)} copy(bf16[24,2,16,1024]{3,2,1,0:T(8,128)(2,1)S(1)} %exchange.1) | data formatting | bytes 3145728

commit v2 on v1

--- a/solution.py
+++ b/solution.py
@@ -20,6 +20,7 @@
 J = 8
 CL = 24
 PL = 2
+OB = 8
 H = CL * XL
 
 
@@ -41,7 +42,7 @@
     yt = _bf(np.stack([np.cos(ang) * sc, -np.sin(ang) * sc], 1).reshape(2 * M, N))
     wgt = np.where(ky == 0, 1.0, 2.0)[:, None]
     g = np.stack([wgt * np.cos(ang) * sc, -wgt * np.sin(ang) * sc], 1).reshape(2 * M, N)
-    g2 = np.concatenate(_split(g), 0)
+    g2 = np.concatenate(_split(g * math.sqrt(0.5)), 0)
 
     k = np.arange(M)
     s = np.arange(S)
@@ -91,18 +92,18 @@
     return lax.dot_general(a, b, (((1,), (1,)), ((), ())), preferred_element_type=F32)
 
 
-NAMES = ("yt", "d2", "tf", "bt", "ex", "ee", "g2")
+NAMES = ("yt", "d2", "tf", "bt", "ex", "ee")
 
 
 def exchange_kernel(*refs):
     nt = len(NAMES)
     field_h, w_h, bias_h = refs[:3]
     tabs_h = refs[3:3 + nt]
-    out_h = refs[3 + nt]
-    fbuf, wbuf, bias_s = refs[4 + nt:7 + nt]
-    tabs = dict(zip(NAMES, refs[7 + nt:7 + 2 * nt]))
+    g2_h, half_h, back_h, g2_o, bias_o = refs[3 + nt:8 + nt]
+    fbuf, wbuf, bias_s = refs[8 + nt:11 + nt]
+    tabs = dict(zip(NAMES, refs[11 + nt:11 + 2 * nt]))
     (send1, recv1, ags, agr, send2, recv2, obuf,
-     in_sem, loc_sem, s1, r1, sa, ra, s2, r2, out_sem) = refs[7 + 2 * nt:]
+     g2, bias_v, in_sem, loc_sem, s1, r1, sa, ra, s2, r2, out_sem) = refs[11 + 2 * nt:]
 
     me = lax.axis_index("gx")
     mc = lax.axis_index("col")
@@ -112,7 +113,8 @@
     rest = [pltpu.make_async_copy(h, tabs[n], in_sem.at[5 + i])
             for i, (h, n) in enumerate(zip(tabs_h[1:], NAMES[1:]))]
     rest += [pltpu.make_async_copy(w_h, wbuf, in_sem.at[3]),
-             pltpu.make_async_copy(bias_h, bias_s, in_sem.at[4])]
+             pltpu.make_async_copy(bias_h, bias_s, in_sem.at[4]),
+             pltpu.make_async_copy(g2_h, g2, in_sem.at[10])]
     for c in first:
         c.start()
 
@@ -240,57 +242,95 @@
     for p in range(PL):
         drain(*ports1[p])
         column_bytes(p).wait_send()
-    g2 = tabs["g2"]
-    ob = 8
-    puts = []
-    for p in range(PL):
-        arrive(*ports2[p])
-        got = recv2[p].reshape(2 * S, H)
-        got = jnp.concatenate([got, got], 0)
-        for n in range(CL // ob):
-            v = lax.dot_general(got[:, 128 * n:128 * n + 128], g2[...], (((0,), (0,)), ((), ())),
-                                preferred_element_type=F32)
-            for i in range(ob):
-                o = n * ob + i
-                u = v[XL * i:XL * i + XL] + bias_s[o]
-                u = 0.5 * u * (1.0 + lax.erf(u * math.sqrt(0.5)))
-                obuf[p, o] = u.astype(BF)
-            put = pltpu.make_async_copy(
-                obuf.at[p, pl.ds(n * ob, ob)], out_h.at[pl.ds(n * ob, ob), p], out_sem.at[p, n])
-            put.start()
-            puts.append(put)
+    for o in range(CL):
+        bias_v[o] = jnp.full((XL, 128), bias_s[o] * math.sqrt(0.5), F32)
+    puts = [pltpu.make_async_copy(g2, g2_o, out_sem.at[0]),
+            pltpu.make_async_copy(bias_v, bias_o, out_sem.at[1])]
+    for put in puts:
+        put.start()
+    arrive(*ports2[0])
+    finish_plane(recv2[0], g2, bias_v, obuf)
+    puts.append(pltpu.make_async_copy(obuf, half_h, out_sem.at[2]))
+    puts[-1].start()
     for p in range(PL):
         drain(*ports2[p])
     for put in puts:
         put.wait()
+    arrive(*ports2[1])
+    put = pltpu.make_async_copy(recv2.at[1], back_h, out_sem.at[3])
+    put.start()
+    put.wait()
+
+
+def finish_plane(msgs, g2, bias_v, obuf, done=None):
+    got = msgs.reshape(2 * S, H)
+    got = jnp.concatenate([got, got], 0)
+    for n in range(CL // OB):
+        v = lax.dot_general(got[:, 128 * n:128 * n + 128], g2[...], (((0,), (0,)), ((), ())),
+                            preferred_element_type=F32)
+        for i in range(OB):
+            o = n * OB + i
+            u = v[XL * i:XL * i + XL] + jnp.concatenate([bias_v[o]] * (N // 128), 1)
+            t = u * math.sqrt(0.5)
+            obuf[o] = (t + t * lax.erf(u)).astype(BF)
+        if done is not None:
+            done(n)
+
+
+def finish_kernel(half_h, back_ref, g2_ref, bias_ref, out_h, obuf, sem):
+    first = pltpu.make_async_copy(half_h, out_h.at[:, 0], sem.at[CL // OB])
+    first.start()
+
+    def put(n):
+        rows = pl.ds(n * OB, OB)
+        return pltpu.make_async_copy(obuf.at[rows], out_h.at[rows, 1], sem.at[n])
+
+    finish_plane(back_ref[...], g2_ref, bias_ref, obuf, lambda n: put(n).start())
+    for n in range(CL // OB):
+        put(n).wait()
+    first.wait()
+
+
+def finish(half, back, g2, bias_v):
+    return pl.pallas_call(
+        finish_kernel,
+        out_shape=jax.ShapeDtypeStruct((CL, PL, XL, N), BF),
+        in_specs=[pl.BlockSpec(memory_space=pl.ANY)] + [pl.BlockSpec(memory_space=pltpu.VMEM)] * 3,
+        out_specs=pl.BlockSpec(memory_space=pl.ANY),
+        scratch_shapes=[pltpu.VMEM((CL, XL, N), BF), pltpu.SemaphoreType.DMA((CL // OB + 1,))],
+        compiler_params=pltpu.CompilerParams(vmem_limit_bytes=24 * 2**20),
+        name="finish",
+    )(half, back, g2, bias_v)
 
 
 def exchanges(field, w, bias, tabs):
     ops = [tabs[n] for n in NAMES]
+    g2 = tabs["g2"]
     vm = [pltpu.VMEM((PL, CL, XL, N), BF), pltpu.VMEM((M * 2 * CL, J * CL), BF), pltpu.SMEM((CL,), F32)]
     vm += [pltpu.VMEM(t.shape, t.dtype) for t in ops]
     msg = pltpu.VMEM((PL, S, 2, H), BF)
     dma = pltpu.SemaphoreType.DMA
     return pl.pallas_call(
         exchange_kernel,
-        out_shape=jax.ShapeDtypeStruct((CL, PL, XL, N), BF),
-        in_specs=[pl.BlockSpec(memory_space=pl.ANY)] * (3 + len(ops)),
-        out_specs=pl.BlockSpec(memory_space=pl.ANY),
+        out_shape=[jax.ShapeDtypeStruct((CL, XL, N), BF), jax.ShapeDtypeStruct((S, 2, H), BF),
+                   jax.ShapeDtypeStruct(g2.shape, BF), jax.ShapeDtypeStruct((CL, XL, 128), F32)],
+        in_specs=[pl.BlockSpec(memory_space=pl.ANY)] * (4 + len(ops)),
+        out_specs=[pl.BlockSpec(memory_space=pl.ANY)] * 4,
         scratch_shapes=vm + [
             msg, msg, pltpu.VMEM((PL, CL, 2 * M), BF), pltpu.VMEM((PL, J, CL, 2 * M), BF), msg, msg,
-            pltpu.VMEM((PL, CL, XL, N), BF),
-            dma((4 + len(ops),)), dma,
-            dma((PL,)), dma((PL,)), dma((PL,)), dma((PL,)), dma((PL,)), dma((PL,)), dma((PL, 3))],
+            pltpu.VMEM((CL, XL, N), BF), pltpu.VMEM(g2.shape, BF), pltpu.VMEM((CL, XL, 128), F32),
+            dma((5 + len(ops),)), dma,
+            dma((PL,)), dma((PL,)), dma((PL,)), dma((PL,)), dma((PL,)), dma((PL,)), dma((4,))],
         compiler_params=pltpu.CompilerParams(
             collective_id=0, has_side_effects=True, vmem_limit_bytes=24 * 2**20),
         name="exchange",
-    )(*[pltpu.with_memory_space_constraint(v, pltpu.HBM) for v in (field, w, bias, *ops)])
+    )(*[pltpu.with_memory_space_constraint(v, pltpu.HBM) for v in (field, w, bias, *ops, g2)])
 
 
 def body(field, weights, bias):
     tabs = {n: jnp.asarray(t) for n, t in tables().items()}
     w = jnp.swapaxes(weights, 3, 4).reshape(M * 2 * CL, J * CL)
-    return exchanges(field, w, bias, tabs)
+    return finish(*exchanges(field, w, bias, tabs))
 
 
 def solution(mesh):

time: 49.9 us -> 49.1 us (0.984)
  local copies, waits for them, and re-layouts: 1.15 us -> 0 us
    unnamed x1 -> x0, local copies, waits for them, and re-layouts: 1.15 us -> none
    pallas_call x1 -> x2, Pallas kernels: 48.6 us -> 49 us  [the longest x1 47.7 us: exchanges(): pl.pallas_call(exchange_kernel, out_shape=[jax.ShapeDtypeStruct((CL, XL,...]
where the time goes in v2:
time: 49.1 us; the launch traced here: 49 us
  Pallas kernels  49 us (100%)
    pallas_call x1, Pallas kernels, exchanges(): pl.pallas_call(exchange_kernel, out_shape=[jax.ShapeDtypeStruct((CL, XL,...  47.7 us
    pallas_call x1, Pallas kernels, finish(): pl.pallas_call(finish_kernel, out_shape=jax.ShapeDtypeStruct((CL, PL, XL,...  1.29 us

profile of v2, /device:TPU:1, one launch (start us, length us, event | category | flops | bytes accessed | tf_op | source)
XLA Modules:
  0.0 49.0 jit_solution(3823253884143441820)
XLA Ops:
  0.0 47.7 %exchange.1 = (bf16[24,16,1024]{2,1,0:T(8,128)(2,1)S(1)}, bf16[64,2,384]{2,1,0:T(2,128)(2,1)S(1)}, bf16[256,1024]{1,0:T(8,128)(2,1)S(1)}, f32[24,16,128]{2,1,0:T(8,128)S(1)}) custom-call(bf16[24,2,16,1024]{3,2,1,0:T(8,128)(2,1)} %refs_0_.1, bf16[3072,192]{1,0:T(8,128)(2,1)} %bitcast.3, f32[24]{0:T(128)} %refs_2_.1, ...), custom_call_target="tpu_custom_call" | custom-call | tf_op jit(solution)/shard_map/exchange/pallas_call | solution.py:313
  47.7 1.3 %finish.1 = bf16[24,2,16,1024]{3,2,1,0:T(8,128)(2,1)} custom-call(bf16[24,16,1024]{2,1,0:T(8,128)(2,1)S(1)} %get-tuple-element.9.half_h, bf16[64,2,384]{2,1,0:T(2,128)(2,1)S(1)} %get-tuple-element.10.back_ref, bf16[256,1024]{1,0:T(8,128)(2,1)S(1)} %get-tuple-element.11.g2_ref, f32[24,16,128]{2,1,0:T(8,128)S(1)} %get-tuple-element.12.bias_ref), custom_call_target="tpu_custom_call" | custom-call | tf_op jit(solution)/shard_map/finish/pallas_call | solution.py:295

commit v3 on v2

--- a/solution.py
+++ b/solution.py
@@ -180,7 +180,7 @@
         return send.at[p], recv.at[p], ssem.at[p], rsem.at[p]
 
     ports1 = [port(send1, recv1, s1, r1, p) for p in range(PL)]
-    ports2 = [port(send2, recv2, s2, r2, p) for p in range(PL)]
+    ports2 = [(send2.at[p], land, s2.at[p], r2.at[p]) for p, land in enumerate((recv2, back_h))]
 
     def columns(p):
         own = pltpu.make_async_copy(ags.at[p], agr.at[p, mc], loc_sem)
@@ -249,7 +249,7 @@
     for put in puts:
         put.start()
     arrive(*ports2[0])
-    finish_plane(recv2[0], g2, bias_v, obuf)
+    finish_plane(recv2[...], g2, bias_v, obuf)
     puts.append(pltpu.make_async_copy(obuf, half_h, out_sem.at[2]))
     puts[-1].start()
     for p in range(PL):
@@ -257,9 +257,6 @@
     for put in puts:
         put.wait()
     arrive(*ports2[1])
-    put = pltpu.make_async_copy(recv2.at[1], back_h, out_sem.at[3])
-    put.start()
-    put.wait()
 
 
 def finish_plane(msgs, g2, bias_v, obuf, done=None):
@@ -317,10 +314,10 @@
         in_specs=[pl.BlockSpec(memory_space=pl.ANY)] * (4 + len(ops)),
         out_specs=[pl.BlockSpec(memory_space=pl.ANY)] * 4,
         scratch_shapes=vm + [
-            msg, msg, pltpu.VMEM((PL, CL, 2 * M), BF), pltpu.VMEM((PL, J, CL, 2 * M), BF), msg, msg,
+            msg, msg, pltpu.VMEM((PL, CL, 2 * M), BF), pltpu.VMEM((PL, J, CL, 2 * M), BF), msg, pltpu.VMEM((S, 2, H), BF),
             pltpu.VMEM((CL, XL, N), BF), pltpu.VMEM(g2.shape, BF), pltpu.VMEM((CL, XL, 128), F32),
             dma((5 + len(ops),)), dma,
-            dma((PL,)), dma((PL,)), dma((PL,)), dma((PL,)), dma((PL,)), dma((PL,)), dma((4,))],
+            dma((PL,)), dma((PL,)), dma((PL,)), dma((PL,)), dma((PL,)), dma((PL,)), dma((3,))],
         compiler_params=pltpu.CompilerParams(
             collective_id=0, has_side_effects=True, vmem_limit_bytes=24 * 2**20),
         name="exchange",

time: 49.1 us -> 49 us (level)
  no operation moved by 1% of the time
where the time goes in v3:
time: 49 us; the launch traced here: 48.9 us
  Pallas kernels  48.9 us (100%)
    pallas_call x1, Pallas kernels, exchanges(): pl.pallas_call(exchange_kernel, out_shape=[jax.ShapeDtypeStruct((CL, XL,...  47.6 us
    pallas_call x1, Pallas kernels, finish(): pl.pallas_call(finish_kernel, out_shape=jax.ShapeDtypeStruct((CL, PL, XL,...  1.29 us

profile of v3, /device:TPU:1, one launch (start us, length us, event | category | flops | bytes accessed | tf_op | source)
XLA Modules:
  0.0 48.9 jit_solution(12962176338697321259)
XLA Ops:
  0.0 47.6 %exchange.1 = (bf16[24,16,1024]{2,1,0:T(8,128)(2,1)S(1)}, bf16[64,2,384]{2,1,0:T(2,128)(2,1)S(1)}, bf16[256,1024]{1,0:T(8,128)(2,1)S(1)}, f32[24,16,128]{2,1,0:T(8,128)S(1)}) custom-call(bf16[24,2,16,1024]{3,2,1,0:T(8,128)(2,1)} %refs_0_.1, bf16[3072,192]{1,0:T(8,128)(2,1)} %bitcast.3, f32[24]{0:T(128)} %refs_2_.1, ...), custom_call_target="tpu_custom_call" | custom-call | tf_op jit(solution)/shard_map/exchange/pallas_call | solution.py:310
  47.6 1.3 %finish.1 = bf16[24,2,16,1024]{3,2,1,0:T(8,128)(2,1)} custom-call(bf16[24,16,1024]{2,1,0:T(8,128)(2,1)S(1)} %get-tuple-element.9.half_h, bf16[64,2,384]{2,1,0:T(2,128)(2,1)S(1)} %get-tuple-element.10.back_ref, bf16[256,1024]{1,0:T(8,128)(2,1)S(1)} %get-tuple-element.11.g2_ref, f32[24,16,128]{2,1,0:T(8,128)S(1)} %get-tuple-element.12.bias_ref), custom_call_target="tpu_custom_call" | custom-call | tf_op jit(solution)/shard_map/finish/pallas_call | solution.py:292

commit v4 on v3

--- a/solution.py
+++ b/solution.py
@@ -103,7 +103,7 @@
     fbuf, wbuf, bias_s = refs[8 + nt:11 + nt]
     tabs = dict(zip(NAMES, refs[11 + nt:11 + 2 * nt]))
     (send1, recv1, ags, agr, send2, recv2, obuf,
-     g2, bias_v, in_sem, loc_sem, s1, r1, sa, ra, s2, r2, out_sem) = refs[11 + 2 * nt:]
+     g2, bias_v, in_sem, loc_sem, s1, r1, sa, ra, s2, r2, out_sem, own_sem) = refs[11 + 2 * nt:]
 
     me = lax.axis_index("gx")
     mc = lax.axis_index("col")
@@ -183,17 +183,22 @@
     ports2 = [(send2.at[p], land, s2.at[p], r2.at[p]) for p, land in enumerate((recv2, back_h))]
 
     def columns(p):
-        own = pltpu.make_async_copy(ags.at[p], agr.at[p, mc], loc_sem)
+        own = pltpu.make_async_copy(ags.at[p], agr.at[p, mc], own_sem.at[p])
         own.start()
 
-        def one(i, _):
+        def to(t):
             pltpu.make_async_remote_copy(
                 src_ref=ags.at[p], dst_ref=agr.at[p, mc], send_sem=sa.at[p], recv_sem=ra.at[p],
-                device_id={"col": lax.rem(mc + i, J)}, device_id_type=MESH).start()
+                device_id={"col": lax.rem(t, J)}, device_id_type=MESH).start()
+
+        to(mc + J // 2)
+
+        def pair(i, _):
+            to(mc + J // 2 - i)
+            to(mc + J // 2 + i)
             return 0
 
-        lax.fori_loop(1, J, one, 0)
-        own.wait()
+        lax.fori_loop(1, J // 2, pair, 0)
 
     def column_bytes(p):
         every = agr.at[p, pl.ds(0, J - 1)]
@@ -223,6 +228,7 @@
     ts = jnp.concatenate([ts, ts], 0)
     for p in range(PL):
         column_bytes(p).wait_recv()
+        pltpu.make_async_copy(ags.at[p], agr.at[p, mc], own_sem.at[p]).wait()
         a = agr[p].reshape(J * CL, 2 * M)
         mixed = jnp.zeros((2 * CL, 2 * M), F32)
         for kg in range(8):
@@ -317,7 +323,7 @@
             msg, msg, pltpu.VMEM((PL, CL, 2 * M), BF), pltpu.VMEM((PL, J, CL, 2 * M), BF), msg, pltpu.VMEM((S, 2, H), BF),
             pltpu.VMEM((CL, XL, N), BF), pltpu.VMEM(g2.shape, BF), pltpu.VMEM((CL, XL, 128), F32),
             dma((5 + len(ops),)), dma,
-            dma((PL,)), dma((PL,)), dma((PL,)), dma((PL,)), dma((PL,)), dma((PL,)), dma((3,))],
+            dma((PL,)), dma((PL,)), dma((PL,)), dma((PL,)), dma((PL,)), dma((PL,)), dma((3,)), dma((PL,))],
         compiler_params=pltpu.CompilerParams(
             collective_id=0, has_side_effects=True, vmem_limit_bytes=24 * 2**20),
         name="exchange",

time: 49 us -> 49.1 us (level)
  no operation moved by 1% of the time
where the time goes in v4:
time: 49.1 us; the launch traced here: 49 us
  Pallas kernels  49 us (100%)
    pallas_call x1, Pallas kernels, exchanges(): pl.pallas_call(exchange_kernel, out_shape=[jax.ShapeDtypeStruct((CL, XL,...  47.7 us
    pallas_call x1, Pallas kernels, finish(): pl.pallas_call(finish_kernel, out_shape=jax.ShapeDtypeStruct((CL, PL, XL,...  1.29 us

profile of v4, /device:TPU:1, one launch (start us, length us, event | category | flops | bytes accessed | tf_op | source)
XLA Modules:
  0.0 49.0 jit_solution(13353193665570392553)
XLA Ops:
  0.0 47.7 %exchange.1 = (bf16[24,16,1024]{2,1,0:T(8,128)(2,1)S(1)}, bf16[64,2,384]{2,1,0:T(2,128)(2,1)S(1)}, bf16[256,1024]{1,0:T(8,128)(2,1)S(1)}, f32[24,16,128]{2,1,0:T(8,128)S(1)}) custom-call(bf16[24,2,16,1024]{3,2,1,0:T(8,128)(2,1)} %refs_0_.1, bf16[3072,192]{1,0:T(8,128)(2,1)} %bitcast.3, f32[24]{0:T(128)} %refs_2_.1, ...), custom_call_target="tpu_custom_call" | custom-call | tf_op jit(solution)/shard_map/exchange/pallas_call | solution.py:316
  47.7 1.3 %finish.1 = bf16[24,2,16,1024]{3,2,1,0:T(8,128)(2,1)} custom-call(bf16[24,16,1024]{2,1,0:T(8,128)(2,1)S(1)} %get-tuple-element.9.half_h, bf16[64,2,384]{2,1,0:T(2,128)(2,1)S(1)} %get-tuple-element.10.back_ref, bf16[256,1024]{1,0:T(8,128)(2,1)S(1)} %get-tuple-element.11.g2_ref, f32[24,16,128]{2,1,0:T(8,128)S(1)} %get-tuple-element.12.bias_ref), custom_call_target="tpu_custom_call" | custom-call | tf_op jit(solution)/shard_map/finish/pallas_call | solution.py:298
